TPU v7x, 32 devices: a whole 2x2x4 slice. The times are simulated.
32 devices in a mesh: aa: 4 (over z), ba: 8 (over y, x, core).
Axes of the slice: x: 2, y: 2, z: 4, core: 2. Of those that a mesh axis runs over, the one named last changes fastest.
Arguments:
- feats: bfloat16 [4, 32, 128, 256], P('aa', 'ba'), may hold values from -6 to 6
- conv_one: bfloat16 [3, 3, 3, 256, 256], replicated, may hold values from -0.078125 to 0.078125
- bias_one: float32 [256], replicated, may hold values from -3 to 3
- conv_two: bfloat16 [3, 3, 3, 256, 256], replicated, may hold values from -0.078125 to 0.078125
- bias_two: float32 [256], replicated, may hold values from -3 to 3
- patch_weight: bfloat16 [2, 2, 256, 128], replicated, may hold values from -0.1875 to 0.1875
- patch_bias: float32 [128], replicated, may hold values from -3 to 3
- embed_weight: bfloat16 [128, 2048], replicated, may hold values from -0.5 to 0.5
- embed_bias: float32 [2048], replicated, may hold values from -6 to 6
- norm_gain: float32 [2048], replicated, may hold values from 0.1 to 1.9
- w_query: bfloat16 [2048, 2048], P(None, 'ba'), may hold values from -2 to 2
- w_key: bfloat16 [2048, 2048], P(None, 'ba'), may hold values from -2 to 2
- w_value: bfloat16 [2048, 2048], P(None, 'ba'), may hold values from -0.125 to 0.125
- w_velocity: bfloat16 [2048, 128], P('ba'), may hold values from -0.5 to 0.5
Outputs:
- velocity: float32 [4096, 128], P(('aa', 'ba'))
All inputs are finite; a program needn't handle non-finite values.
Results may differ from a plain program's by a relative error of at most 0.035.
Values may be sent and summed in bfloat16 or wider, within the bound.
A program may use at most 128 MiB of HBM per device.

v0:
```python
import math
import jax
import jax.numpy as jnp
from jax import lax
from jax.sharding import PartitionSpec as P

HEAD_DIM = 64


def with_halo(cells, sides, width):
    for axis, dim in sides:
        count = lax.axis_size(axis)
        ends = count - 1
        head = lax.slice_in_dim(cells, 0, width, axis=dim)
        tail = lax.slice_in_dim(cells, cells.shape[dim] - width, cells.shape[dim], axis=dim)
        cells = jnp.concatenate(
            [
                lax.ppermute(tail, axis, [(i, (i + 1) % count) for i in range(ends)]),
                cells,
                lax.ppermute(head, axis, [((i + 1) % count, i) for i in range(ends)]),
            ],
            axis=dim,
        )
    return cells


def convolve(field, kernel, bias):
    frames, rows, width, chans = field.shape
    padded = with_halo(field, (("aa", 0), ("ba", 1)), 1)
    padded = jnp.pad(padded, ((0, 0), (0, 0), (1, 1), (0, 0)))
    total = jnp.zeros((frames * rows * width, kernel.shape[-1]), jnp.float32)
    for shift_t in range(3):
        for shift_r in range(3):
            window = padded[shift_t : shift_t + frames, shift_r : shift_r + rows]
            stacked = jnp.concatenate(
                [window[:, :, shift_w : shift_w + width] for shift_w in range(3)], axis=-1
            )
            total = total + jnp.dot(
                stacked.reshape(-1, 3 * chans),
                kernel[shift_t, shift_r].reshape(3 * chans, -1),
                preferred_element_type=jnp.float32,
            )
    return (total + bias).reshape(frames, rows, width, -1)


def patchify(field, weight, bias):
    frames, rows, width, chans = field.shape
    blocks = (
        field.reshape(frames, rows // 2, 2, width // 2, 2, chans)
        .transpose(0, 1, 3, 2, 4, 5)
        .reshape(-1, 4 * chans)
    )
    return (
        jnp.dot(blocks, weight.reshape(4 * chans, -1), preferred_element_type=jnp.float32) + bias
    ).astype(jnp.bfloat16)


def normalize(latent_rows, embed_weight, embed_bias, norm_gain):
    hidden = jnp.dot(latent_rows, embed_weight, preferred_element_type=jnp.float32) + embed_bias
    center = hidden - hidden.mean(-1, keepdims=True)
    spread = (center * center).mean(-1, keepdims=True)
    return (center * lax.rsqrt(spread + 1e-05) * norm_gain).astype(jnp.bfloat16)


def attend(queries, keys, values):
    rows, width = queries.shape
    heads = width // HEAD_DIM
    scale = HEAD_DIM ** (-0.5)
    query_heads = queries.reshape(rows, heads, HEAD_DIM)
    start_state = (
        jnp.full((heads, rows), -jnp.inf, jnp.float32),
        jnp.zeros((heads, rows), jnp.float32),
        jnp.zeros((rows, heads, HEAD_DIM), jnp.float32),
    )
    key_rows = lax.all_gather(keys, "aa", axis=0, tiled=True)
    value_rows = lax.all_gather(values, "aa", axis=0, tiled=True)
    count = key_rows.shape[0]
    block = math.gcd(count, 1024)

    def one_step(index, state):
        best, denom, accum = state
        key_block = lax.dynamic_slice_in_dim(key_rows, index * block, block, 0).reshape(
            block, heads, HEAD_DIM
        )
        value_block = lax.dynamic_slice_in_dim(value_rows, index * block, block, 0).reshape(
            block, heads, HEAD_DIM
        )
        scores = (
            jnp.einsum("qhd,khd->hqk", query_heads, key_block, preferred_element_type=jnp.float32)
            * scale
        )
        peak = jnp.maximum(best, scores.max(-1))
        probs = jnp.exp(scores - peak[..., None])
        fade = jnp.exp(best - peak)
        denom = denom * fade + probs.sum(-1)
        accum = accum * fade.T[..., None] + jnp.einsum(
            "hqk,khd->qhd",
            probs.astype(jnp.bfloat16),
            value_block,
            preferred_element_type=jnp.float32,
        )
        return (peak, denom, accum)

    best, denom, accum = lax.fori_loop(0, count // block, one_step, start_state)
    return (accum / denom.T[..., None]).reshape(rows, width).astype(jnp.bfloat16)


def on_device(
    feats,
    conv_one,
    bias_one,
    conv_two,
    bias_two,
    patch_weight,
    patch_bias,
    embed_weight,
    embed_bias,
    norm_gain,
    w_query,
    w_key,
    w_value,
    w_velocity,
):
    first = jax.nn.gelu(convolve(feats, conv_one, bias_one), approximate=False).astype(jnp.bfloat16)
    second = (
        first.astype(jnp.float32)
        + jax.nn.gelu(convolve(first, conv_two, bias_two), approximate=False)
    ).astype(jnp.bfloat16)
    latents = patchify(second, patch_weight, patch_bias)
    width = w_query.shape[1]
    w_joined = jnp.concatenate([w_query, w_key, w_value], axis=1)
    joined = jnp.dot(
        normalize(
            lax.all_gather(latents, "ba", axis=0, tiled=True), embed_weight, embed_bias, norm_gain
        ),
        w_joined,
        preferred_element_type=jnp.float32,
    ).astype(jnp.bfloat16)
    attended = attend(joined[:, :width], joined[:, width : 2 * width], joined[:, 2 * width :])
    return lax.psum_scatter(
        jnp.dot(attended, w_velocity, preferred_element_type=jnp.float32).astype(jnp.bfloat16),
        "ba",
        scatter_dimension=0,
        tiled=True,
    ).astype(jnp.float32)


def solution(mesh):
    return jax.shard_map(
        on_device,
        mesh=mesh,
        in_specs=(
            P("aa", "ba", None, None),
            P(),
            P(),
            P(),
            P(),
            P(),
            P(),
            P(),
            P(),
            P(),
            P(None, "ba"),
            P(None, "ba"),
            P(None, "ba"),
            P("ba", None),
        ),
        out_specs=P(("aa", "ba"), None),
        check_vma=False,
    )
```

profile of v0, /device:TPU:0, one launch (start us, length us, event | category | flops | bytes accessed | tf_op | source)
XLA Modules:
  0.0 332.6 jit_solution(549942878547130094)
XLA Ops:
  6.5 5.1 %collective-permute-start = (bf16[1,4,128,256]{3,2,1,0:T(8,128)(2,1)}, bf16[1,4,128,256]{3,2,1,0:T(8,128)(2,1)S(1)}, u32[]{:S(2)}, u32[]{:S(2)}) collective-permute-start(bf16[1,4,128,256]{3,2,1,0:T(8,128)(2,1)} %param.16), channel_id=1, source_target_pairs={{0,8},{8,16},{16,24},{1,9},{9,17},{17,25},{2,10},{10,18},{18,26},{... | collective-permute-start | bytes 786440 | tf_op jit(solution)/shard_map/ppermute | solution.py:18
  11.6 1.3 collective-permute-start.1
  12.9 4.5 %collective-permute-done = bf16[1,4,128,256]{3,2,1,0:T(8,128)(2,1)S(1)} collective-permute-done((bf16[1,4,128,256]{3,2,1,0:T(8,128)(2,1)}, bf16[1,4,128,256]{3,2,1,0:T(8,128)(2,1)S(1)}, u32[]{:S(2)}, u32[]{:S(2)}) %collective-permute-start) | collective-permute-done | bytes 262176 | tf_op jit(solution)/shard_map/ppermute | solution.py:18
  17.5 1.0 constant_dynamic-update-slice_fusion.1
  18.5 3.0 collective-permute-done.1
  21.6 1.3 collective-permute-start.2
  22.9 1.3 collective-permute-start.3
  24.2 2.2 fusion.102
  26.4 1.6 collective-permute-done.3
  27.9 0.6 select_maximum_fusion.5
  28.5 0.9 fusion.105
  30.6 0.4 convolution_add_fusion.15
  32.5 0.4 convolution_add_fusion.10
  33.6 2.1 fusion.69
  35.7 1.1 fusion.66
  36.8 3.5 %collective-permute-start.4 = (bf16[1,4,128,256]{3,2,1,0:T(8,128)(2,1)S(1)}, bf16[1,4,128,256]{3,2,1,0:T(8,128)(2,1)S(1)}, u32[]{:S(2)}, u32[]{:S(2)}) collective-permute-start(bf16[1,4,128,256]{3,2,1,0:T(8,128)(2,1)S(1)} %fusion.66), channel_id=1, source_target_pairs={{0,8},{8,16},{16,24},{1,9},{9,17},{17,25},{2,10},{10,18},{18,26},{... | collective-permute-start | bytes 786440 | tf_op jit(solution)/shard_map/ppermute | solution.py:18
  40.3 1.3 collective-permute-start.5
  41.6 2.6 collective-permute-done.4
  44.1 4.4 %collective-permute-done.5 = bf16[1,4,128,256]{3,2,1,0:T(8,128)(2,1)S(1)} collective-permute-done((bf16[1,4,128,256]{3,2,1,0:T(8,128)(2,1)S(1)}, bf16[1,4,128,256]{3,2,1,0:T(8,128)(2,1)S(1)}, u32[]{:S(2)}, u32[]{:S(2)}) %collective-permute-start.5) | collective-permute-done | bytes 262176 | tf_op jit(solution)/shard_map/ppermute | solution.py:20
  48.5 0.8 pad_maximum_fusion.29
  49.3 5.3 %collective-permute-start.6 = (bf16[3,1,128,256]{3,2,1,0:T(8,128)(2,1)}, bf16[3,1,128,256]{3,2,1,0:T(8,128)(2,1)}, u32[]{:S(2)}, u32[]{:S(2)}) collective-permute-start(bf16[3,1,128,256]{3,2,1,0:T(8,128)(2,1)} %get-tuple-element.246), channel_id=1, source_target_pairs={{0,1},{1,2},{2,3},{3,4},{4,5},{5,6},{6,7},{8,9},{9,10},{10,11},{11... | collective-permute-start | bytes 589832 | tf_op jit(solution)/shard_map/ppermute | solution.py:18
  54.6 1.5 collective-permute-start.7
  56.1 1.7 fusion.101
  58.4 1.2 collective-permute-done.7
  59.6 1.5 select_maximum_fusion.1
  61.1 0.8 fusion.104
  62.0 1.1 fusion.35
  63.6 0.5 copy-done.8
  64.8 0.7 copy-done.7
  66.3 0.6 copy-done.11
  67.8 0.6 copy-done.4
  68.8 0.5 copy-done.3
  69.7 0.4 broadcast_multiply_fusion
  70.8 2.2 fusion.98
  73.5 1.2 fusion.31
  74.7 15.0 %all_gather.9 = bf16[1024,128]{1,0:T(8,128)(2,1)S(1)} all-gather(bf16[128,128]{1,0:T(8,128)(2,1)S(1)} %fusion.31), channel_id=1, replica_groups=mesh['aa'=4,'ba'=8] {'ba'}, dimensions={0}, use_global_device_ids=true | all-gather | bytes 294912 | tf_op jit(solution)/shard_map/all_gather | solution.py:134
  89.7 1.3 add_reduce_fusion
  91.0 1.2 multiply_reduce_fusion
  92.9 4.3 %fusion.25 = bf16[1024,768]{0,1:T(8,128)(2,1)S(1)} fusion(bf16[2048,256]{1,0:T(8,128)(2,1)S(1)} %copy-done.16, bf16[2048,256]{1,0:T(8,128)(2,1)S(1)} %copy-done.17, bf16[2048,256]{1,0:T(8,128)(2,1)S(1)} %copy-done.18, f32[1024,2048]{1,0:T(8,128)S(1)} %get-tuple-element.255, f32[2048]{0:T(1024)S(1)} %copy-done.19, f32[1024]{0:T(1024)S(1)} %add_rsqrt_fusion, ...), kind=kOutput, calls=%fused_computation.33 | convolution fusion | flops 3241934848 | bytes 13131776 | tf_op jit(solution)/shard_map/dot_general | solution.py:132
  97.2 1.1 fusion.103
  98.3 0.7 all-gather.5.cloned.1.call-update
  99.4 43.0 %all-gather.3.cloned.1.call-done = bf16[4096,256]{0,1:T(8,128)(2,1)} async-done(((bf16[1024,256]{0,1:T(8,128)(2,1)}), bf16[4096,256]{0,1:T(8,128)(2,1)}) %all-gather.3.cloned.1.call-update) | async-done | bytes 2097168 | tf_op jit(solution)/shard_map/all_gather | solution.py:75
  142.4 46.1 %all-gather.5.cloned.1.call-done = bf16[4096,256]{0,1:T(8,128)(2,1)} async-done(((bf16[1024,256]{0,1:T(8,128)(2,1)}), bf16[4096,256]{0,1:T(8,128)(2,1)}) %all-gather.5.cloned.1.call-update) | async-done | bytes 2097168 | tf_op jit(solution)/shard_map/all_gather | solution.py:76
  188.4 101.7 %while.18 = (s32[]{:T(128)}, f32[4,1024]{1,0:T(4,128)S(1)}, f32[4,1024]{1,0:T(4,128)S(1)}, f32[1024,4,64]{0,2,1:T(8,128)S(1)}, bf16[4096,256]{0,1:T(8,128)(2,1)}...) while((s32[]{:T(128)}, f32[4,1024]{1,0:T(4,128)S(1)}, ...), condition=%wide.region_5.6_spmd.clone, body=%wide.region_2.5_spmd.clone.sunk | while | flops 1108107264 | bytes 56361128 | solution.py:104
  188.4 1.3 constant_dynamic-slice_fusion.3
  189.7 8.1 %bitcast_reduce_fusion.2 = (f32[4,1024]{1,0:T(4,128)S(1)}, f32[4,1024,1024]{2,1,0:T(8,128)}) fusion(bf16[1024,4,64]{0,2,1:T(8,128)(2,1)S(1)} %bitcast.131, bf16[1024,4,64]{0,2,1:T(8,128)(2,1)S(1)} %get-tuple-element.340), kind=kOutput, calls=%fused_computation.1.clone.1 | convolution fusion | flops 545255424 | bytes 17842176 | tf_op jit(solution)/shard_map/while/body/eval_jaxpr/qhd,khd->hqk/dot_general | solution.py:89
  197.9 7.4 %fusion.168 = f32[1024,4,64]{0,2,1:T(8,128)S(1)} fusion(bf16[1024,4,64]{0,2,1:T(8,128)(2,1)S(1)} %bitcast.132, f32[4,1024,1024]{2,1,0:T(8,128)} %get-tuple-element.310, f32[4,1024]{1,0:T(4,128)S(1)} %get-tuple-element.336, f32[1024,4,64]{0,2,1:T(8,128)S(1)} %get-tuple-element.327, f32[1024,4]{0,1:T(4,128)S(1)} %get-tuple-element.312, pred[]{:T(512)S(6)} %compare.43), kind=kOutput, calls=%fused_computation.7.clone.1 | convolution fusion | flops 550240256 | bytes 19431424 | tf_op jit(solution)/shard_map/while/body/eval_jaxpr/hqk,khd->qhd/dot_general | solution.py:96
  205.2 8.5 %fusion.166 = f32[4,1024]{1,0:T(4,128)S(1)} fusion(f32[4,1024,1024]{2,1,0:T(8,128)} %get-tuple-element.310, f32[4,1024]{1,0:T(4,128)S(1)} %get-tuple-element.336), kind=kLoop, calls=%fused_computation.4.clone.1 | loop fusion | flops 12578816 | bytes 16809984 | tf_op jit(solution)/shard_map/while/body/eval_jaxpr/reduce_sum | solution.py:95
  213.8 1.3 constant_dynamic-slice_fusion.3
  215.1 8.1 %bitcast_reduce_fusion.2 = (f32[4,1024]{1,0:T(4,128)S(1)}, f32[4,1024,1024]{2,1,0:T(8,128)}) fusion(bf16[1024,4,64]{0,2,1:T(8,128)(2,1)S(1)} %bitcast.131, bf16[1024,4,64]{0,2,1:T(8,128)(2,1)S(1)} %get-tuple-element.340), kind=kOutput, calls=%fused_computation.1.clone.1 | convolution fusion | flops 545255424 | bytes 17842176 | tf_op jit(solution)/shard_map/while/body/eval_jaxpr/qhd,khd->hqk/dot_general | solution.py:89
  223.3 7.4 %fusion.168 = f32[1024,4,64]{0,2,1:T(8,128)S(1)} fusion(bf16[1024,4,64]{0,2,1:T(8,128)(2,1)S(1)} %bitcast.132, f32[4,1024,1024]{2,1,0:T(8,128)} %get-tuple-element.310, f32[4,1024]{1,0:T(4,128)S(1)} %get-tuple-element.336, f32[1024,4,64]{0,2,1:T(8,128)S(1)} %get-tuple-element.327, f32[1024,4]{0,1:T(4,128)S(1)} %get-tuple-element.312, pred[]{:T(512)S(6)} %compare.43), kind=kOutput, calls=%fused_computation.7.clone.1 | convolution fusion | flops 550240256 | bytes 19431424 | tf_op jit(solution)/shard_map/while/body/eval_jaxpr/hqk,khd->qhd/dot_general | solution.py:96
  230.7 8.5 %fusion.166 = f32[4,1024]{1,0:T(4,128)S(1)} fusion(f32[4,1024,1024]{2,1,0:T(8,128)} %get-tuple-element.310, f32[4,1024]{1,0:T(4,128)S(1)} %get-tuple-element.336), kind=kLoop, calls=%fused_computation.4.clone.1 | loop fusion | flops 12578816 | bytes 16809984 | tf_op jit(solution)/shard_map/while/body/eval_jaxpr/reduce_sum | solution.py:95
  239.3 1.3 constant_dynamic-slice_fusion.3
  240.5 8.1 %bitcast_reduce_fusion.2 = (f32[4,1024]{1,0:T(4,128)S(1)}, f32[4,1024,1024]{2,1,0:T(8,128)}) fusion(bf16[1024,4,64]{0,2,1:T(8,128)(2,1)S(1)} %bitcast.131, bf16[1024,4,64]{0,2,1:T(8,128)(2,1)S(1)} %get-tuple-element.340), kind=kOutput, calls=%fused_computation.1.clone.1 | convolution fusion | flops 545255424 | bytes 17842176 | tf_op jit(solution)/shard_map/while/body/eval_jaxpr/qhd,khd->hqk/dot_general | solution.py:89
  248.7 7.4 %fusion.168 = f32[1024,4,64]{0,2,1:T(8,128)S(1)} fusion(bf16[1024,4,64]{0,2,1:T(8,128)(2,1)S(1)} %bitcast.132, f32[4,1024,1024]{2,1,0:T(8,128)} %get-tuple-element.310, f32[4,1024]{1,0:T(4,128)S(1)} %get-tuple-element.336, f32[1024,4,64]{0,2,1:T(8,128)S(1)} %get-tuple-element.327, f32[1024,4]{0,1:T(4,128)S(1)} %get-tuple-element.312, pred[]{:T(512)S(6)} %compare.43), kind=kOutput, calls=%fused_computation.7.clone.1 | convolution fusion | flops 550240256 | bytes 19431424 | tf_op jit(solution)/shard_map/while/body/eval_jaxpr/hqk,khd->qhd/dot_general | solution.py:96
  256.1 8.5 %fusion.166 = f32[4,1024]{1,0:T(4,128)S(1)} fusion(f32[4,1024,1024]{2,1,0:T(8,128)} %get-tuple-element.310, f32[4,1024]{1,0:T(4,128)S(1)} %get-tuple-element.336), kind=kLoop, calls=%fused_computation.4.clone.1 | loop fusion | flops 12578816 | bytes 16809984 | tf_op jit(solution)/shard_map/while/body/eval_jaxpr/reduce_sum | solution.py:95
  264.7 1.3 constant_dynamic-slice_fusion.3
  266.0 8.1 %bitcast_reduce_fusion.2 = (f32[4,1024]{1,0:T(4,128)S(1)}, f32[4,1024,1024]{2,1,0:T(8,128)}) fusion(bf16[1024,4,64]{0,2,1:T(8,128)(2,1)S(1)} %bitcast.131, bf16[1024,4,64]{0,2,1:T(8,128)(2,1)S(1)} %get-tuple-element.340), kind=kOutput, calls=%fused_computation.1.clone.1 | convolution fusion | flops 545255424 | bytes 17842176 | tf_op jit(solution)/shard_map/while/body/eval_jaxpr/qhd,khd->hqk/dot_general | solution.py:89
  274.1 7.4 %fusion.168 = f32[1024,4,64]{0,2,1:T(8,128)S(1)} fusion(bf16[1024,4,64]{0,2,1:T(8,128)(2,1)S(1)} %bitcast.132, f32[4,1024,1024]{2,1,0:T(8,128)} %get-tuple-element.310, f32[4,1024]{1,0:T(4,128)S(1)} %get-tuple-element.336, f32[1024,4,64]{0,2,1:T(8,128)S(1)} %get-tuple-element.327, f32[1024,4]{0,1:T(4,128)S(1)} %get-tuple-element.312, pred[]{:T(512)S(6)} %compare.43), kind=kOutput, calls=%fused_computation.7.clone.1 | convolution fusion | flops 550240256 | bytes 19431424 | tf_op jit(solution)/shard_map/while/body/eval_jaxpr/hqk,khd->qhd/dot_general | solution.py:96
  281.5 8.5 %fusion.166 = f32[4,1024]{1,0:T(4,128)S(1)} fusion(f32[4,1024,1024]{2,1,0:T(8,128)} %get-tuple-element.310, f32[4,1024]{1,0:T(4,128)S(1)} %get-tuple-element.336), kind=kLoop, calls=%fused_computation.4.clone.1 | loop fusion | flops 12578816 | bytes 16809984 | tf_op jit(solution)/shard_map/while/body/eval_jaxpr/reduce_sum | solution.py:95
  290.2 0.7 copy-done.13
  290.9 1.0 convolution_convert_fusion
  292.0 32.6 %reduce-scatter.2.cloned.1.call-done = bf16[128,128]{1,0:T(8,128)(2,1)} async-done(((bf16[1024,128]{1,0:T(8,128)(2,1)}), bf16[128,128]{1,0:T(8,128)(2,1)}) %reduce-scatter.2.cloned.1.call-update) | async-done | bytes 32784 | tf_op jit(solution)/shard_map/reduce_scatter | solution.py:140
  324.6 1.4 convert_element_type.90
  (92 shorter events, 9.8 us)
Async XLA Ops:
  6.5 83.1 %copy-start = (bf16[128,2048]{1,0:T(8,128)(2,1)S(1)}, bf16[128,2048]{1,0:T(8,128)(2,1)}, u32[]{:S(2)}) copy-start(bf16[128,2048]{1,0:T(8,128)(2,1)} %param.23) | copy-start | bytes 1572868
  6.5 135.8 %all-gather.3.cloned.1.call-start = ((), (), s32[]{:S(2)}) async-start(), calls=%async_computation.1 | async-start | bytes 2621440 | tf_op jit(solution)/shard_map/all_gather | solution.py:75
  6.5 10.9 %collective-permute-start = (bf16[1,4,128,256]{3,2,1,0:T(8,128)(2,1)}, bf16[1,4,128,256]{3,2,1,0:T(8,128)(2,1)S(1)}, u32[]{:S(2)}, u32[]{:S(2)}) collective-permute-start(bf16[1,4,128,256]{3,2,1,0:T(8,128)(2,1)} %param.16), channel_id=1, source_target_pairs={{0,8},{8,16},{16,24},{1,9},{9,17},{17,25},{2,10},{10,18},{18,26},{... | collective-permute-start | bytes 786440 | tf_op jit(solution)/shard_map/ppermute | solution.py:18
  11.6 9.9 %collective-permute-start.1 = (bf16[1,4,128,256]{3,2,1,0:T(8,128)(2,1)}, bf16[1,4,128,256]{3,2,1,0:T(8,128)(2,1)S(1)}, u32[]{:S(2)}, u32[]{:S(2)}) collective-permute-start(bf16[1,4,128,256]{3,2,1,0:T(8,128)(2,1)} %param.16), channel_id=1, source_target_pairs={{8,0},{16,8},{24,16},{9,1},{17,9},{25,17},{10,2},{18,10},{26,18},{... | collective-permute-start | bytes 786440 | tf_op jit(solution)/shard_map/ppermute | solution.py:20
  21.6 4.8 %collective-permute-start.2 = (bf16[3,1,128,256]{3,2,1,0:T(8,128)(2,1)S(1)}, bf16[3,1,128,256]{3,2,1,0:T(8,128)(2,1)S(1)}, u32[]{:S(2)}, u32[]{:S(2)}) collective-permute-start(bf16[3,1,128,256]{3,2,1,0:T(8,128)(2,1)S(1)} %get-tuple-element.248), channel_id=1, source_target_pairs={{0,1},{1,2},{2,3},{3,4},{4,5},{5,6},{6,7},{8,9},{9,10},{10,11},{11... | collective-permute-start | bytes 589832 | tf_op jit(solution)/shard_map/ppermute | solution.py:18
  22.9 5.1 %collective-permute-start.3 = (bf16[3,1,128,256]{3,2,1,0:T(8,128)(2,1)S(1)}, bf16[3,1,128,256]{3,2,1,0:T(8,128)(2,1)S(1)}, u32[]{:S(2)}, u32[]{:S(2)}) collective-permute-start(bf16[3,1,128,256]{3,2,1,0:T(8,128)(2,1)S(1)} %get-tuple-element.247), channel_id=1, source_target_pairs={{1,0},{2,1},{3,2},{4,3},{5,4},{6,5},{7,6},{9,8},{10,9},{11,10},{12... | collective-permute-start | bytes 589832 | tf_op jit(solution)/shard_map/ppermute | solution.py:20
  28.5 1.0 copy-start.10
  32.9 0.7 copy-start.20
  33.6 22.5 %copy-start.2 = (bf16[3,3,3,256,256]{4,3,2,1,0:T(8,128)(2,1)S(1)}, bf16[3,3,3,256,256]{4,3,2,1,0:T(8,128)(2,1)}, u32[]{:S(2)}) copy-start(bf16[3,3,3,256,256]{4,3,2,1,0:T(8,128)(2,1)} %param.19) | copy-start | bytes 10616836
  36.8 7.3 %collective-permute-start.4 = (bf16[1,4,128,256]{3,2,1,0:T(8,128)(2,1)S(1)}, bf16[1,4,128,256]{3,2,1,0:T(8,128)(2,1)S(1)}, u32[]{:S(2)}, u32[]{:S(2)}) collective-permute-start(bf16[1,4,128,256]{3,2,1,0:T(8,128)(2,1)S(1)} %fusion.66), channel_id=1, source_target_pairs={{0,8},{8,16},{16,24},{1,9},{9,17},{17,25},{2,10},{10,18},{18,26},{... | collective-permute-start | bytes 786440 | tf_op jit(solution)/shard_map/ppermute | solution.py:18
  40.3 8.3 %collective-permute-start.5 = (bf16[1,4,128,256]{3,2,1,0:T(8,128)(2,1)S(1)}, bf16[1,4,128,256]{3,2,1,0:T(8,128)(2,1)S(1)}, u32[]{:S(2)}, u32[]{:S(2)}) collective-permute-start(bf16[1,4,128,256]{3,2,1,0:T(8,128)(2,1)S(1)} %fusion.66), channel_id=1, source_target_pairs={{8,0},{16,8},{24,16},{9,1},{17,9},{25,17},{10,2},{18,10},{26,18},{... | collective-permute-start | bytes 786440 | tf_op jit(solution)/shard_map/ppermute | solution.py:20
  49.3 9.1 %collective-permute-start.6 = (bf16[3,1,128,256]{3,2,1,0:T(8,128)(2,1)}, bf16[3,1,128,256]{3,2,1,0:T(8,128)(2,1)}, u32[]{:S(2)}, u32[]{:S(2)}) collective-permute-start(bf16[3,1,128,256]{3,2,1,0:T(8,128)(2,1)} %get-tuple-element.246), channel_id=1, source_target_pairs={{0,1},{1,2},{2,3},{3,4},{4,5},{5,6},{6,7},{8,9},{9,10},{10,11},{11... | collective-permute-start | bytes 589832 | tf_op jit(solution)/shard_map/ppermute | solution.py:18
  54.6 5.0 %collective-permute-start.7 = (bf16[3,1,128,256]{3,2,1,0:T(8,128)(2,1)}, bf16[3,1,128,256]{3,2,1,0:T(8,128)(2,1)S(1)}, u32[]{:S(2)}, u32[]{:S(2)}) collective-permute-start(bf16[3,1,128,256]{3,2,1,0:T(8,128)(2,1)} %get-tuple-element.245), channel_id=1, source_target_pairs={{1,0},{2,1},{3,2},{4,3},{5,4},{6,5},{7,6},{9,8},{10,9},{11,10},{12... | collective-permute-start | bytes 589832 | tf_op jit(solution)/shard_map/ppermute | solution.py:20
  62.0 1.1 copy-start.9
  63.1 1.0 copy-start.8
  64.5 1.0 copy-start.7
  64.8 1.1 copy-start.6
  65.9 1.0 copy-start.11
  65.9 1.1 copy-start.21
  66.3 1.1 copy-start.5
  67.3 1.0 copy-start.4
  68.3 1.0 copy-start.3
  68.7 1.0 copy-start.14
  70.8 2.7 copy-start.15
  70.8 18.9 %copy-start.12 = (f32[2048]{0:T(1024)S(1)}, f32[2048]{0:T(1024)}, u32[]{:S(2)}) copy-start(f32[2048]{0:T(1024)} %param.24) | copy-start | bytes 24580
  91.0 1.3 copy-start.16
  91.0 1.5 copy-start.17
  91.0 1.8 copy-start.18
  91.0 1.8 copy-start.19
  98.3 90.1 %all-gather.5.cloned.1.call-start = ((), (), s32[]{:S(2)}) async-start(), calls=%async_computation.2 | async-start | bytes 2621440 | tf_op jit(solution)/shard_map/all_gather | solution.py:76
  99.1 225.6 %reduce-scatter.2.cloned.1.call-start = ((), (), s32[]{:S(2)}) async-start(), calls=%async_computation.3 | async-start | bytes 294912 | tf_op jit(solution)/shard_map/reduce_scatter | solution.py:140
  290.1 0.8 copy-start.13
  290.1 35.9 %copy-start.1 = (bf16[128,2048]{1,0:T(8,128)(2,1)S(1)}, bf16[128,2048]{1,0:T(8,128)(2,1)}, u32[]{:S(2)}) copy-start(bf16[128,2048]{1,0:T(8,128)(2,1)} %param.23) | copy-start | bytes 1572868
Sparse Core Ops, SparseCore 0:
  98.4 43.8 all-gather.2
  143.9 44.4 all-gather.4
  292.1 32.4 reduce-scatter.1
where the time goes:
time: 334 us; the launch traced here: 333 us
  waiting for transfers between devices  140 us (42%)
  matrix products  78.4 us (23%)
  other arithmetic  45.5 us (14%)
  starting transfers between devices  20.9 us (6%)
  local copies, waits for them, and re-layouts  19.1 us (6%)
  blocking collectives  15 us (4%)
  between operations  13.7 us (4%)
    all_gather x1, waiting for transfers between devices, attend(): value_rows = lax.all_gather(values, 'aa', axis=0, tiled=True)  46.1 us
    all_gather x1, waiting for transfers between devices, attend(): key_rows = lax.all_gather(keys, 'aa', axis=0, tiled=True)  43 us
    reduce_sum x4, other arithmetic, one_step(): denom = denom * fade + probs.sum(-1)  34.1 us
    reduce_scatter x1, waiting for transfers between devices, on_device(): lax.psum_scatter(jnp.dot(attended, w_velocity, preferred_element_type=jnp...  32.6 us
    dot_general x4, matrix products, one_step(): jnp.einsum('qhd,khd->hqk', query_heads, key_block, preferred_element_type...  32.6 us
    dot_general x4, matrix products, one_step(): jnp.einsum('hqk,khd->qhd', probs.astype(jnp.bfloat16), value_block, prefe...  29.5 us
    ppermute x4, starting transfers between devices, with_halo(): lax.ppermute(tail, axis, [(i, (i + 1) % count) for i in range(ends)])  15.2 us
    all_gather x1, blocking collectives, on_device(): lax.all_gather(latents, 'ba', axis=0, tiled=True)  15 us
  transfers between devices with their start and end apart: 11, of which 9 were waited for; matrix products, arithmetic and copies ran while one was open for 2% of the time, Pallas kernels for 0%

commit v1 on v0

--- a/solution.py
+++ b/solution.py
@@ -73,7 +73,16 @@
         jnp.zeros((rows, heads, HEAD_DIM), jnp.float32),
     )
     key_rows = lax.all_gather(keys, "aa", axis=0, tiled=True)
-    value_rows = lax.all_gather(values, "aa", axis=0, tiled=True)
+    ways = lax.axis_size("aa")
+    up = [(d, (d + 1) % ways) for d in range(ways)]
+    down = [(d, (d - 1) % ways) for d in range(ways)]
+    earlier, later = ([values], [values])
+    for _ in range(ways // 2):
+        earlier.append(lax.ppermute(earlier[-1], "aa", up))
+    for _ in range((ways - 1) // 2):
+        later.append(lax.ppermute(later[-1], "aa", down))
+    line = jnp.concatenate([*earlier[::-1], *later[1:]], axis=0)
+    value_rows = jnp.roll(line, (lax.axis_index("aa") - ways // 2) * values.shape[0], axis=0)
     count = key_rows.shape[0]
     block = math.gcd(count, 1024)
 

time: 334 us -> 330 us (0.988)
  waiting for transfers between devices: 140 us -> 126 us
  local copies, waits for them, and re-layouts: 19.1 us -> 25.2 us
  starting transfers between devices: 20.9 us -> 26.3 us
    all_gather x1 -> x0, waiting for transfers between devices: 46.1 us -> none  [attend(): value_rows = lax.all_gather(values, 'aa', axis=0, tiled=True)]
    ppermute x0 -> x3, waiting for transfers between devices: none -> 35 us  [the longest x2 27.2 us: attend(): earlier.append(lax.ppermute(earlier[-1], 'aa', up))]
    ppermute x0 -> x3, starting transfers between devices: none -> 5.45 us  [the longest x1 3.82 us: attend(): later.append(lax.ppermute(later[-1], 'aa', down))]
    unnamed x46 -> x61, local copies, waits for them, and re-layouts: 5.63 us -> 8.73 us
  transfers between devices with their start and end apart: 11 -> 13, of which waited for: 9 -> 11; matrix products, arithmetic and copies ran while one was open for 2% -> 3% of each run, Pallas kernels for 0% -> 0%
where the time goes in v1:
time: 330 us; the launch traced here: 329 us
  waiting for transfers between devices  126 us (38%)
  matrix products  77.5 us (23%)
  other arithmetic  45.5 us (14%)
  starting transfers between devices  26.3 us (8%)
  local copies, waits for them, and re-layouts  25.2 us (8%)
  blocking collectives  15 us (5%)
  between operations  14.2 us (4%)
    all_gather x1, waiting for transfers between devices, attend(): key_rows = lax.all_gather(keys, 'aa', axis=0, tiled=True)  40.5 us
    reduce_sum x4, other arithmetic, one_step(): denom = denom * fade + probs.sum(-1)  34.1 us
    reduce_scatter x1, waiting for transfers between devices, on_device(): lax.psum_scatter(jnp.dot(attended, w_velocity, preferred_element_type=jnp...  32.6 us
    dot_general x4, matrix products, one_step(): jnp.einsum('qhd,khd->hqk', query_heads, key_block, preferred_element_type...  32.6 us
    dot_general x4, matrix products, one_step(): jnp.einsum('hqk,khd->qhd', probs.astype(jnp.bfloat16), value_block, prefe...  29.5 us
    ppermute x2, waiting for transfers between devices, attend(): earlier.append(lax.ppermute(earlier[-1], 'aa', up))  27.2 us
    ppermute x4, starting transfers between devices, with_halo(): lax.ppermute(tail, axis, [(i, (i + 1) % count) for i in range(ends)])  15.2 us
    all_gather x1, blocking collectives, on_device(): lax.all_gather(latents, 'ba', axis=0, tiled=True)  15 us
  transfers between devices with their start and end apart: 13, of which 11 were waited for; matrix products, arithmetic and copies ran while one was open for 3% of the time, Pallas kernels for 0%

profile of v1, /device:TPU:0, one launch (start us, length us, event | category | flops | bytes accessed | tf_op | source)
XLA Modules:
  0.0 329.4 jit_solution(3581667895422941268)
XLA Ops:
  6.5 5.1 %collective-permute-start = (bf16[1,4,128,256]{3,2,1,0:T(8,128)(2,1)}, bf16[1,4,128,256]{3,2,1,0:T(8,128)(2,1)S(1)}, u32[]{:S(2)}, u32[]{:S(2)}) collective-permute-start(bf16[1,4,128,256]{3,2,1,0:T(8,128)(2,1)} %param.16), channel_id=1, source_target_pairs={{0,8},{8,16},{16,24},{1,9},{9,17},{17,25},{2,10},{10,18},{18,26},{... | collective-permute-start | bytes 786440 | tf_op jit(solution)/shard_map/ppermute | solution.py:18
  11.6 1.3 collective-permute-start.1
  12.9 4.5 %collective-permute-done = bf16[1,4,128,256]{3,2,1,0:T(8,128)(2,1)S(1)} collective-permute-done((bf16[1,4,128,256]{3,2,1,0:T(8,128)(2,1)}, bf16[1,4,128,256]{3,2,1,0:T(8,128)(2,1)S(1)}, u32[]{:S(2)}, u32[]{:S(2)}) %collective-permute-start) | collective-permute-done | bytes 262176 | tf_op jit(solution)/shard_map/ppermute | solution.py:18
  17.5 1.0 constant_dynamic-update-slice_fusion.1
  18.5 3.0 collective-permute-done.1
  21.6 1.3 collective-permute-start.2
  22.9 1.3 collective-permute-start.3
  24.2 2.2 fusion.102
  26.4 1.6 collective-permute-done.3
  27.9 0.6 select_maximum_fusion.5
  28.5 0.9 fusion.104
  33.5 2.1 fusion.69
  35.7 1.1 fusion.66
  36.8 3.5 %collective-permute-start.4 = (bf16[1,4,128,256]{3,2,1,0:T(8,128)(2,1)S(1)}, bf16[1,4,128,256]{3,2,1,0:T(8,128)(2,1)S(1)}, u32[]{:S(2)}, u32[]{:S(2)}) collective-permute-start(bf16[1,4,128,256]{3,2,1,0:T(8,128)(2,1)S(1)} %fusion.66), channel_id=1, source_target_pairs={{0,8},{8,16},{16,24},{1,9},{9,17},{17,25},{2,10},{10,18},{18,26},{... | collective-permute-start | bytes 786440 | tf_op jit(solution)/shard_map/ppermute | solution.py:18
  40.3 1.3 collective-permute-start.5
  41.6 2.6 collective-permute-done.4
  44.1 4.4 %collective-permute-done.5 = bf16[1,4,128,256]{3,2,1,0:T(8,128)(2,1)S(1)} collective-permute-done((bf16[1,4,128,256]{3,2,1,0:T(8,128)(2,1)S(1)}, bf16[1,4,128,256]{3,2,1,0:T(8,128)(2,1)S(1)}, u32[]{:S(2)}, u32[]{:S(2)}) %collective-permute-start.5) | collective-permute-done | bytes 262176 | tf_op jit(solution)/shard_map/ppermute | solution.py:20
  48.5 0.8 pad_maximum_fusion.29
  49.3 5.3 %collective-permute-start.6 = (bf16[3,1,128,256]{3,2,1,0:T(8,128)(2,1)}, bf16[3,1,128,256]{3,2,1,0:T(8,128)(2,1)}, u32[]{:S(2)}, u32[]{:S(2)}) collective-permute-start(bf16[3,1,128,256]{3,2,1,0:T(8,128)(2,1)} %get-tuple-element.246), channel_id=1, source_target_pairs={{0,1},{1,2},{2,3},{3,4},{4,5},{5,6},{6,7},{8,9},{9,10},{10,11},{11... | collective-permute-start | bytes 589832 | tf_op jit(solution)/shard_map/ppermute | solution.py:18
  54.6 1.5 collective-permute-start.7
  56.1 1.6 fusion.101
  58.4 1.3 collective-permute-done.7
  59.7 1.6 select_maximum_fusion.1
  61.2 0.9 fusion.103
  62.1 1.1 fusion.35
  65.0 0.7 copy-done.8
  66.4 0.6 copy-done.14
  67.9 0.6 copy-done.5
  70.9 2.2 fusion.98
  73.8 15.0 %all_gather.6 = bf16[1024,128]{1,0:T(8,128)(2,1)S(1)} all-gather(bf16[128,128]{1,0:T(8,128)(2,1)S(1)} %fusion.31), channel_id=1, replica_groups=mesh['aa'=4,'ba'=8] {'ba'}, dimensions={0}, use_global_device_ids=true | all-gather | bytes 294912 | tf_op jit(solution)/shard_map/all_gather | solution.py:143
  88.9 1.3 add_reduce_fusion
  90.2 1.2 multiply_reduce_fusion
  92.1 4.3 %fusion.25 = bf16[1024,768]{0,1:T(8,128)(2,1)S(1)} fusion(bf16[2048,256]{1,0:T(8,128)(2,1)S(1)} %copy-done.20, bf16[2048,256]{1,0:T(8,128)(2,1)S(1)} %copy-done.21, bf16[2048,256]{1,0:T(8,128)(2,1)S(1)} %copy-done.22, f32[1024,2048]{1,0:T(8,128)S(1)} %get-tuple-element.255, f32[2048]{0:T(1024)S(1)} %copy-done.23, f32[1024]{0:T(1024)S(1)} %add_rsqrt_fusion, ...), kind=kOutput, calls=%fused_computation.33 | convolution fusion | flops 3241934848 | bytes 13131776 | tf_op jit(solution)/shard_map/dot_general | solution.py:141
  96.4 1.6 collective-permute-start.8
  98.0 14.4 %collective-permute-done.8 = bf16[1024,256]{0,1:T(8,128)(2,1)S(1)} collective-permute-done((bf16[1024,256]{0,1:T(8,128)(2,1)S(1)}, bf16[1024,256]{0,1:T(8,128)(2,1)S(1)}, u32[]{:S(2)}, u32[]{:S(2)}) %collective-permute-start.8) | collective-permute-done | bytes 524320 | tf_op jit(solution)/shard_map/ppermute | solution.py:81
  112.4 3.8 %collective-permute-start.10 = (bf16[1024,256]{0,1:T(8,128)(2,1)S(1)}, bf16[1024,256]{0,1:T(8,128)(2,1)S(1)}, u32[]{:S(2)}, u32[]{:S(2)}) collective-permute-start(bf16[1024,256]{0,1:T(8,128)(2,1)S(1)} %slice.446), channel_id=1, source_target_pairs={{0,24},{8,0},{16,8},{24,16},{1,25},{9,1},{17,9},{25,17},{2,26},{10... | collective-permute-start | bytes 1572872 | tf_op jit(solution)/shard_map/ppermute | solution.py:83
  116.3 12.8 %collective-permute-done.9 = bf16[1024,256]{0,1:T(8,128)(2,1)S(1)} collective-permute-done((bf16[1024,256]{0,1:T(8,128)(2,1)S(1)}, bf16[1024,256]{0,1:T(8,128)(2,1)S(1)}, u32[]{:S(2)}, u32[]{:S(2)}) %collective-permute-start.9) | collective-permute-done | bytes 524320 | tf_op jit(solution)/shard_map/ppermute | solution.py:81
  129.2 7.8 %collective-permute-done.10 = bf16[1024,256]{0,1:T(8,128)(2,1)S(1)} collective-permute-done((bf16[1024,256]{0,1:T(8,128)(2,1)S(1)}, bf16[1024,256]{0,1:T(8,128)(2,1)S(1)}, u32[]{:S(2)}, u32[]{:S(2)}) %collective-permute-start.10) | collective-permute-done | bytes 524320 | tf_op jit(solution)/shard_map/ppermute | solution.py:83
  137.1 0.9 constant_dynamic-update-slice_fusion.4
  138.1 2.0 copy-done.3
  140.4 0.9 constant_dynamic-update-slice_fusion.3
  141.3 3.1 constant_dynamic-slice_fusion.2
  144.5 40.5 %all-gather.2.cloned.1.call-done = bf16[4096,256]{0,1:T(8,128)(2,1)} async-done(((bf16[1024,256]{0,1:T(8,128)(2,1)}), bf16[4096,256]{0,1:T(8,128)(2,1)}) %all-gather.2.cloned.1.call-update) | async-done | bytes 2097168 | tf_op jit(solution)/shard_map/all_gather | solution.py:75
  184.9 101.7 %while.18 = (s32[]{:T(128)}, f32[4,1024]{1,0:T(4,128)S(1)}, f32[4,1024]{1,0:T(4,128)S(1)}, f32[1024,4,64]{0,2,1:T(8,128)S(1)}, bf16[4096,256]{0,1:T(8,128)(2,1)}...) while((s32[]{:T(128)}, f32[4,1024]{1,0:T(4,128)S(1)}, ...), condition=%wide.region_5.6_spmd.clone, body=%wide.region_2.5_spmd.clone.sunk | while | flops 1108107264 | bytes 56361128 | solution.py:113
  184.9 1.3 constant_dynamic-slice_fusion.4
  186.2 8.1 %bitcast_reduce_fusion.2 = (f32[4,1024]{1,0:T(4,128)S(1)}, f32[4,1024,1024]{2,1,0:T(8,128)}) fusion(bf16[1024,4,64]{0,2,1:T(8,128)(2,1)S(1)} %bitcast.131, bf16[1024,4,64]{0,2,1:T(8,128)(2,1)S(1)} %get-tuple-element.340), kind=kOutput, calls=%fused_computation.1.clone.1 | convolution fusion | flops 545255424 | bytes 17842176 | tf_op jit(solution)/shard_map/while/body/eval_jaxpr/qhd,khd->hqk/dot_general | solution.py:98
  194.4 7.4 %fusion.167 = f32[1024,4,64]{0,2,1:T(8,128)S(1)} fusion(bf16[1024,4,64]{0,2,1:T(8,128)(2,1)S(1)} %bitcast.132, f32[4,1024,1024]{2,1,0:T(8,128)} %get-tuple-element.310, f32[4,1024]{1,0:T(4,128)S(1)} %get-tuple-element.336, f32[1024,4,64]{0,2,1:T(8,128)S(1)} %get-tuple-element.327, f32[1024,4]{0,1:T(4,128)S(1)} %get-tuple-element.312, pred[]{:T(512)S(6)} %compare.44), kind=kOutput, calls=%fused_computation.7.clone.1 | convolution fusion | flops 550240256 | bytes 19431424 | tf_op jit(solution)/shard_map/while/body/eval_jaxpr/hqk,khd->qhd/dot_general | solution.py:105
  201.8 8.5 %fusion.165 = f32[4,1024]{1,0:T(4,128)S(1)} fusion(f32[4,1024,1024]{2,1,0:T(8,128)} %get-tuple-element.310, f32[4,1024]{1,0:T(4,128)S(1)} %get-tuple-element.336), kind=kLoop, calls=%fused_computation.4.clone.1 | loop fusion | flops 12578816 | bytes 16809984 | tf_op jit(solution)/shard_map/while/body/eval_jaxpr/reduce_sum | solution.py:104
  210.4 1.3 constant_dynamic-slice_fusion.4
  211.6 8.1 %bitcast_reduce_fusion.2 = (f32[4,1024]{1,0:T(4,128)S(1)}, f32[4,1024,1024]{2,1,0:T(8,128)}) fusion(bf16[1024,4,64]{0,2,1:T(8,128)(2,1)S(1)} %bitcast.131, bf16[1024,4,64]{0,2,1:T(8,128)(2,1)S(1)} %get-tuple-element.340), kind=kOutput, calls=%fused_computation.1.clone.1 | convolution fusion | flops 545255424 | bytes 17842176 | tf_op jit(solution)/shard_map/while/body/eval_jaxpr/qhd,khd->hqk/dot_general | solution.py:98
  219.8 7.4 %fusion.167 = f32[1024,4,64]{0,2,1:T(8,128)S(1)} fusion(bf16[1024,4,64]{0,2,1:T(8,128)(2,1)S(1)} %bitcast.132, f32[4,1024,1024]{2,1,0:T(8,128)} %get-tuple-element.310, f32[4,1024]{1,0:T(4,128)S(1)} %get-tuple-element.336, f32[1024,4,64]{0,2,1:T(8,128)S(1)} %get-tuple-element.327, f32[1024,4]{0,1:T(4,128)S(1)} %get-tuple-element.312, pred[]{:T(512)S(6)} %compare.44), kind=kOutput, calls=%fused_computation.7.clone.1 | convolution fusion | flops 550240256 | bytes 19431424 | tf_op jit(solution)/shard_map/while/body/eval_jaxpr/hqk,khd->qhd/dot_general | solution.py:105
  227.2 8.5 %fusion.165 = f32[4,1024]{1,0:T(4,128)S(1)} fusion(f32[4,1024,1024]{2,1,0:T(8,128)} %get-tuple-element.310, f32[4,1024]{1,0:T(4,128)S(1)} %get-tuple-element.336), kind=kLoop, calls=%fused_computation.4.clone.1 | loop fusion | flops 12578816 | bytes 16809984 | tf_op jit(solution)/shard_map/while/body/eval_jaxpr/reduce_sum | solution.py:104
  235.8 1.3 constant_dynamic-slice_fusion.4
  237.1 8.1 %bitcast_reduce_fusion.2 = (f32[4,1024]{1,0:T(4,128)S(1)}, f32[4,1024,1024]{2,1,0:T(8,128)}) fusion(bf16[1024,4,64]{0,2,1:T(8,128)(2,1)S(1)} %bitcast.131, bf16[1024,4,64]{0,2,1:T(8,128)(2,1)S(1)} %get-tuple-element.340), kind=kOutput, calls=%fused_computation.1.clone.1 | convolution fusion | flops 545255424 | bytes 17842176 | tf_op jit(solution)/shard_map/while/body/eval_jaxpr/qhd,khd->hqk/dot_general | solution.py:98
  245.2 7.4 %fusion.167 = f32[1024,4,64]{0,2,1:T(8,128)S(1)} fusion(bf16[1024,4,64]{0,2,1:T(8,128)(2,1)S(1)} %bitcast.132, f32[4,1024,1024]{2,1,0:T(8,128)} %get-tuple-element.310, f32[4,1024]{1,0:T(4,128)S(1)} %get-tuple-element.336, f32[1024,4,64]{0,2,1:T(8,128)S(1)} %get-tuple-element.327, f32[1024,4]{0,1:T(4,128)S(1)} %get-tuple-element.312, pred[]{:T(512)S(6)} %compare.44), kind=kOutput, calls=%fused_computation.7.clone.1 | convolution fusion | flops 550240256 | bytes 19431424 | tf_op jit(solution)/shard_map/while/body/eval_jaxpr/hqk,khd->qhd/dot_general | solution.py:105
  252.6 8.5 %fusion.165 = f32[4,1024]{1,0:T(4,128)S(1)} fusion(f32[4,1024,1024]{2,1,0:T(8,128)} %get-tuple-element.310, f32[4,1024]{1,0:T(4,128)S(1)} %get-tuple-element.336), kind=kLoop, calls=%fused_computation.4.clone.1 | loop fusion | flops 12578816 | bytes 16809984 | tf_op jit(solution)/shard_map/while/body/eval_jaxpr/reduce_sum | solution.py:104
  261.2 1.3 constant_dynamic-slice_fusion.4
  262.5 8.1 %bitcast_reduce_fusion.2 = (f32[4,1024]{1,0:T(4,128)S(1)}, f32[4,1024,1024]{2,1,0:T(8,128)}) fusion(bf16[1024,4,64]{0,2,1:T(8,128)(2,1)S(1)} %bitcast.131, bf16[1024,4,64]{0,2,1:T(8,128)(2,1)S(1)} %get-tuple-element.340), kind=kOutput, calls=%fused_computation.1.clone.1 | convolution fusion | flops 545255424 | bytes 17842176 | tf_op jit(solution)/shard_map/while/body/eval_jaxpr/qhd,khd->hqk/dot_general | solution.py:98
  270.6 7.4 %fusion.167 = f32[1024,4,64]{0,2,1:T(8,128)S(1)} fusion(bf16[1024,4,64]{0,2,1:T(8,128)(2,1)S(1)} %bitcast.132, f32[4,1024,1024]{2,1,0:T(8,128)} %get-tuple-element.310, f32[4,1024]{1,0:T(4,128)S(1)} %get-tuple-element.336, f32[1024,4,64]{0,2,1:T(8,128)S(1)} %get-tuple-element.327, f32[1024,4]{0,1:T(4,128)S(1)} %get-tuple-element.312, pred[]{:T(512)S(6)} %compare.44), kind=kOutput, calls=%fused_computation.7.clone.1 | convolution fusion | flops 550240256 | bytes 19431424 | tf_op jit(solution)/shard_map/while/body/eval_jaxpr/hqk,khd->qhd/dot_general | solution.py:105
  278.0 8.5 %fusion.165 = f32[4,1024]{1,0:T(4,128)S(1)} fusion(f32[4,1024,1024]{2,1,0:T(8,128)} %get-tuple-element.310, f32[4,1024]{1,0:T(4,128)S(1)} %get-tuple-element.336), kind=kLoop, calls=%fused_computation.4.clone.1 | loop fusion | flops 12578816 | bytes 16809984 | tf_op jit(solution)/shard_map/while/body/eval_jaxpr/reduce_sum | solution.py:104
  286.7 0.7 copy-done.17
  287.5 1.1 convolution_convert_fusion
  288.5 32.6 %reduce-scatter.2.cloned.1.call-done = bf16[128,128]{1,0:T(8,128)(2,1)} async-done(((bf16[1024,128]{1,0:T(8,128)(2,1)}), bf16[128,128]{1,0:T(8,128)(2,1)}) %reduce-scatter.2.cloned.1.call-update) | async-done | bytes 32784 | tf_op jit(solution)/shard_map/reduce_scatter | solution.py:149
  321.2 1.4 convert_element_type.90
  (112 shorter events, 12.5 us)
Async XLA Ops:
  6.5 82.3 %copy-start = (bf16[128,2048]{1,0:T(8,128)(2,1)S(1)}, bf16[128,2048]{1,0:T(8,128)(2,1)}, u32[]{:S(2)}) copy-start(bf16[128,2048]{1,0:T(8,128)(2,1)} %param.23) | copy-start | bytes 1572868
  6.5 178.4 %all-gather.2.cloned.1.call-start = ((), (), s32[]{:S(2)}) async-start(), calls=%async_computation.1 | async-start | bytes 2621440 | tf_op jit(solution)/shard_map/all_gather | solution.py:75
  6.5 10.9 %collective-permute-start = (bf16[1,4,128,256]{3,2,1,0:T(8,128)(2,1)}, bf16[1,4,128,256]{3,2,1,0:T(8,128)(2,1)S(1)}, u32[]{:S(2)}, u32[]{:S(2)}) collective-permute-start(bf16[1,4,128,256]{3,2,1,0:T(8,128)(2,1)} %param.16), channel_id=1, source_target_pairs={{0,8},{8,16},{16,24},{1,9},{9,17},{17,25},{2,10},{10,18},{18,26},{... | collective-permute-start | bytes 786440 | tf_op jit(solution)/shard_map/ppermute | solution.py:18
  11.6 9.9 %collective-permute-start.1 = (bf16[1,4,128,256]{3,2,1,0:T(8,128)(2,1)}, bf16[1,4,128,256]{3,2,1,0:T(8,128)(2,1)S(1)}, u32[]{:S(2)}, u32[]{:S(2)}) collective-permute-start(bf16[1,4,128,256]{3,2,1,0:T(8,128)(2,1)} %param.16), channel_id=1, source_target_pairs={{8,0},{16,8},{24,16},{9,1},{17,9},{25,17},{10,2},{18,10},{26,18},{... | collective-permute-start | bytes 786440 | tf_op jit(solution)/shard_map/ppermute | solution.py:20
  21.6 4.8 %collective-permute-start.2 = (bf16[3,1,128,256]{3,2,1,0:T(8,128)(2,1)S(1)}, bf16[3,1,128,256]{3,2,1,0:T(8,128)(2,1)S(1)}, u32[]{:S(2)}, u32[]{:S(2)}) collective-permute-start(bf16[3,1,128,256]{3,2,1,0:T(8,128)(2,1)S(1)} %get-tuple-element.248), channel_id=1, source_target_pairs={{0,1},{1,2},{2,3},{3,4},{4,5},{5,6},{6,7},{8,9},{9,10},{10,11},{11... | collective-permute-start | bytes 589832 | tf_op jit(solution)/shard_map/ppermute | solution.py:18
  22.9 5.1 %collective-permute-start.3 = (bf16[3,1,128,256]{3,2,1,0:T(8,128)(2,1)S(1)}, bf16[3,1,128,256]{3,2,1,0:T(8,128)(2,1)S(1)}, u32[]{:S(2)}, u32[]{:S(2)}) collective-permute-start(bf16[3,1,128,256]{3,2,1,0:T(8,128)(2,1)S(1)} %get-tuple-element.247), channel_id=1, source_target_pairs={{1,0},{2,1},{3,2},{4,3},{5,4},{6,5},{7,6},{9,8},{10,9},{11,10},{12... | collective-permute-start | bytes 589832 | tf_op jit(solution)/shard_map/ppermute | solution.py:20
  28.5 1.0 copy-start.11
  32.9 0.7 copy-start.24
  33.5 22.6 %copy-start.2 = (bf16[3,3,3,256,256]{4,3,2,1,0:T(8,128)(2,1)S(1)}, bf16[3,3,3,256,256]{4,3,2,1,0:T(8,128)(2,1)}, u32[]{:S(2)}) copy-start(bf16[3,3,3,256,256]{4,3,2,1,0:T(8,128)(2,1)} %param.19) | copy-start | bytes 10616836
  36.8 7.3 %collective-permute-start.4 = (bf16[1,4,128,256]{3,2,1,0:T(8,128)(2,1)S(1)}, bf16[1,4,128,256]{3,2,1,0:T(8,128)(2,1)S(1)}, u32[]{:S(2)}, u32[]{:S(2)}) collective-permute-start(bf16[1,4,128,256]{3,2,1,0:T(8,128)(2,1)S(1)} %fusion.66), channel_id=1, source_target_pairs={{0,8},{8,16},{16,24},{1,9},{9,17},{17,25},{2,10},{10,18},{18,26},{... | collective-permute-start | bytes 786440 | tf_op jit(solution)/shard_map/ppermute | solution.py:18
  40.3 8.3 %collective-permute-start.5 = (bf16[1,4,128,256]{3,2,1,0:T(8,128)(2,1)S(1)}, bf16[1,4,128,256]{3,2,1,0:T(8,128)(2,1)S(1)}, u32[]{:S(2)}, u32[]{:S(2)}) collective-permute-start(bf16[1,4,128,256]{3,2,1,0:T(8,128)(2,1)S(1)} %fusion.66), channel_id=1, source_target_pairs={{8,0},{16,8},{24,16},{9,1},{17,9},{25,17},{10,2},{18,10},{26,18},{... | collective-permute-start | bytes 786440 | tf_op jit(solution)/shard_map/ppermute | solution.py:20
  49.3 9.0 %collective-permute-start.6 = (bf16[3,1,128,256]{3,2,1,0:T(8,128)(2,1)}, bf16[3,1,128,256]{3,2,1,0:T(8,128)(2,1)}, u32[]{:S(2)}, u32[]{:S(2)}) collective-permute-start(bf16[3,1,128,256]{3,2,1,0:T(8,128)(2,1)} %get-tuple-element.246), channel_id=1, source_target_pairs={{0,1},{1,2},{2,3},{3,4},{4,5},{5,6},{6,7},{8,9},{9,10},{10,11},{11... | collective-permute-start | bytes 589832 | tf_op jit(solution)/shard_map/ppermute | solution.py:18
  54.6 5.0 %collective-permute-start.7 = (bf16[3,1,128,256]{3,2,1,0:T(8,128)(2,1)}, bf16[3,1,128,256]{3,2,1,0:T(8,128)(2,1)S(1)}, u32[]{:S(2)}, u32[]{:S(2)}) collective-permute-start(bf16[3,1,128,256]{3,2,1,0:T(8,128)(2,1)} %get-tuple-element.245), channel_id=1, source_target_pairs={{1,0},{2,1},{3,2},{4,3},{5,4},{6,5},{7,6},{9,8},{10,9},{11,10},{12... | collective-permute-start | bytes 589832 | tf_op jit(solution)/shard_map/ppermute | solution.py:20
  59.7 2.4 copy-start.12
  62.1 1.1 copy-start.10
  63.3 1.0 copy-start.9
  63.6 1.0 copy-start.13
  64.6 1.0 copy-start.8
  64.9 1.1 copy-start.7
  66.0 1.0 copy-start.14
  66.0 1.1 copy-start.25
  66.4 1.0 copy-start.6
  67.5 1.0 copy-start.5
  68.5 1.0 copy-start.4
  68.8 1.0 copy-start.18
  70.9 2.7 copy-start.15
  70.9 2.7 copy-start.19
  70.9 17.9 %copy-start.16 = (f32[2048]{0:T(1024)S(1)}, f32[2048]{0:T(1024)}, u32[]{:S(2)}) copy-start(f32[2048]{0:T(1024)} %param.24) | copy-start | bytes 24580
  90.2 1.3 copy-start.20
  90.2 1.5 copy-start.21
  90.2 1.8 copy-start.22
  90.2 1.8 copy-start.23
  96.4 16.0 %collective-permute-start.8 = (bf16[1024,256]{0,1:T(8,128)(2,1)S(1)}, bf16[1024,256]{0,1:T(8,128)(2,1)S(1)}, u32[]{:S(2)}, u32[]{:S(2)}) collective-permute-start(bf16[1024,256]{0,1:T(8,128)(2,1)S(1)} %slice.446), channel_id=1, source_target_pairs={{0,8},{8,16},{16,24},{24,0},{1,9},{9,17},{17,25},{25,1},{2,10},{10... | collective-permute-start | bytes 1572872 | tf_op jit(solution)/shard_map/ppermute | solution.py:81
  112.4 16.6 %collective-permute-start.9 = (bf16[1024,256]{0,1:T(8,128)(2,1)S(1)}, bf16[1024,256]{0,1:T(8,128)(2,1)S(1)}, u32[]{:S(2)}, u32[]{:S(2)}) collective-permute-start(bf16[1024,256]{0,1:T(8,128)(2,1)S(1)} %collective-permute-done.8), channel_id=1, source_target_pairs={{0,8},{8,16},{16,24},{24,0},{1,9},{9,17},{17,25},{25,1},{2,10},{10... | collective-permute-start | bytes 1572872 | tf_op jit(solution)/shard_map/ppermute | solution.py:81
  112.4 24.6 %collective-permute-start.10 = (bf16[1024,256]{0,1:T(8,128)(2,1)S(1)}, bf16[1024,256]{0,1:T(8,128)(2,1)S(1)}, u32[]{:S(2)}, u32[]{:S(2)}) collective-permute-start(bf16[1024,256]{0,1:T(8,128)(2,1)S(1)} %slice.446), channel_id=1, source_target_pairs={{0,24},{8,0},{16,8},{24,16},{1,25},{9,1},{17,9},{25,17},{2,26},{10... | collective-permute-start | bytes 1572872 | tf_op jit(solution)/shard_map/ppermute | solution.py:83
  138.1 2.0 copy-start.3
  140.0 181.1 %reduce-scatter.2.cloned.1.call-start = ((), (), s32[]{:S(2)}) async-start(), calls=%async_computation.2 | async-start | bytes 294912 | tf_op jit(solution)/shard_map/reduce_scatter | solution.py:149
  286.6 0.8 copy-start.17
  286.6 36.0 %copy-start.1 = (bf16[128,2048]{1,0:T(8,128)(2,1)S(1)}, bf16[128,2048]{1,0:T(8,128)(2,1)}, u32[]{:S(2)}) copy-start(bf16[128,2048]{1,0:T(8,128)(2,1)} %param.23) | copy-start | bytes 1572868
Sparse Core Ops, SparseCore 0:
  140.2 44.7 all-gather.1
  288.7 32.4 reduce-scatter.1
